TPU v7x, 32 devices: a whole 2x2x4 slice. The times are simulated.
32 devices in a mesh: gx: 16 (over z, y, core), gy: 2 (over x).
Axes of the slice: x: 2, y: 2, z: 4, core: 2. Of those that a mesh axis runs over, the one named last changes fastest.
Arguments:
- inputs: bfloat16 [128, 8192], P('gy', 'gx'), may hold values from -6 to 6
- gate_pre: bfloat16 [128, 28672], P('gx', 'gy'), may hold values from -8 to 8
- up_pre: bfloat16 [128, 28672], P('gx', 'gy'), may hold values from -6 to 6
- out_grad: bfloat16 [128, 8192], P('gy', 'gx'), may hold values from -6 to 6
- w_gate: bfloat16 [8192, 28672], P('gx', 'gy'), may hold values from -0.0625 to 0.0625
- w_up: bfloat16 [8192, 28672], P('gx', 'gy'), may hold values from -0.0625 to 0.0625
- w_down: bfloat16 [28672, 8192], P('gy', 'gx'), may hold values from -0.03125 to 0.03125
Outputs:
- grad_input: bfloat16 [128, 8192], P('gy', 'gx')
- grad_w_gate: bfloat16 [8192, 28672], P('gx', 'gy')
- grad_w_up: bfloat16 [8192, 28672], P('gx', 'gy')
- grad_w_down: bfloat16 [28672, 8192], P('gy', 'gx')
All inputs are finite; a program needn't handle non-finite values.
Results may differ from a plain program's by a relative error of at most 0.017.
Values may be sent and summed in bfloat16 or wider, within the bound.
A program may use at most 256 MiB of HBM per device.

v0:
```python
import jax
import jax.numpy as jnp
from jax import lax
from jax.sharding import PartitionSpec as P


def swiglu_back(d_hidden, gate_pre, up_pre):
    gate_val = gate_pre.astype(jnp.float32)
    up_val = up_pre.astype(jnp.float32)
    sig = jax.nn.sigmoid(gate_val)
    silu_val = gate_val * sig
    hidden = (silu_val * up_val).astype(jnp.bfloat16)
    d_up = (d_hidden * silu_val).astype(jnp.bfloat16)
    d_gate = (d_hidden * up_val * sig * (1.0 + gate_val * (1.0 - sig))).astype(jnp.bfloat16)
    return (d_gate, d_up, hidden)


def contract_rows(left, right):
    return lax.dot_general(
        left, right, (((0,), (0,)), ((), ())), preferred_element_type=jnp.float32
    )


def contract_cols(left, right):
    return lax.dot_general(
        left, right, (((1,), (1,)), ((), ())), preferred_element_type=jnp.float32
    )


def per_device(inputs, gate_pre, up_pre, out_grad, w_gate, w_up, w_down):
    input_rows, grad_rows = (
        lax.all_gather(inputs, "gy", axis=0, tiled=True),
        lax.all_gather(out_grad, "gy", axis=0, tiled=True),
    )
    d_hidden = lax.psum_scatter(
        contract_cols(grad_rows, w_down).astype(jnp.bfloat16), "gx", scatter_dimension=0, tiled=True
    ).astype(jnp.float32)
    d_gate, d_up, hidden = swiglu_back(d_hidden, gate_pre, up_pre)
    gate_piece = lax.all_gather(d_gate, "gx", axis=0, tiled=True)
    up_piece = lax.all_gather(d_up, "gx", axis=0, tiled=True)
    hidden_piece = lax.all_gather(hidden, "gx", axis=0, tiled=True)
    gate_total = contract_rows(input_rows, gate_piece)
    up_total = contract_rows(input_rows, up_piece)
    down_total = contract_rows(hidden_piece, grad_rows)
    input_block_grad = contract_cols(gate_piece, w_gate) + contract_cols(up_piece, w_up)
    input_total = input_block_grad
    gate_total, up_total, down_total, input_total = (gate_total, up_total, down_total, input_total)
    grad_input = lax.psum_scatter(
        input_total.astype(jnp.bfloat16), "gy", scatter_dimension=0, tiled=True
    )
    return (
        grad_input,
        gate_total.astype(jnp.bfloat16),
        up_total.astype(jnp.bfloat16),
        down_total.astype(jnp.bfloat16),
    )


def solution(mesh):
    placed = (
        P("gy", "gx"),
        P("gx", "gy"),
        P("gx", "gy"),
        P("gy", "gx"),
        P("gx", "gy"),
        P("gx", "gy"),
        P("gy", "gx"),
    )
    return jax.shard_map(
        per_device,
        mesh=mesh,
        in_specs=placed,
        out_specs=(P("gy", "gx"), P("gx", "gy"), P("gx", "gy"), P("gy", "gx")),
        check_vma=False,
    )
```

profile of v0, /device:TPU:0, one launch (start us, length us, event | category | flops | bytes accessed | tf_op | source)
XLA Modules:
  0.0 300.6 jit_solution(5242010842057136992)
XLA Ops:
  7.2 0.0 copy-start.2
  7.2 0.0 copy-start.1
  7.2 0.0 copy-start.3
  7.2 0.0 reduce-scatter.3.cloned.1.call-start
  7.2 6.2 %all_gather.15 = bf16[128,512]{1,0:T(8,128)(2,1)S(1)} all-gather(bf16[64,512]{1,0:T(8,128)(2,1)} %param.10), channel_id=1, replica_groups=mesh['gx'=16,'gy'=2] {'gy'}, dimensions={0}, use_global_device_ids=true | all-gather | bytes 196608 | tf_op jit(solution)/shard_map/all_gather | solution.py:33
  13.5 11.8 %convolution_convert_fusion.3 = bf16[128,14336]{1,0:T(8,128)(2,1)} fusion(bf16[128,512]{1,0:T(8,128)(2,1)S(1)} %all_gather.15, bf16[14336,512]{1,0:T(8,128)(2,1)} %param.13), kind=kOutput, calls=%fused_computation.5 | convolution fusion | flops 1880883200 | bytes 18481152 | tf_op jit(solution)/shard_map/dot_general | solution.py:25
  25.3 0.0 reduce-scatter.3.cloned.1.call-update
  25.3 0.0 all-gather.4.cloned.1.call-start
  25.4 70.5 %reduce-scatter.3.cloned.1.call-done = bf16[8,14336]{1,0:T(8,128)(2,1)} async-done(((bf16[128,14336]{1,0:T(8,128)(2,1)}), bf16[8,14336]{1,0:T(8,128)(2,1)}) %reduce-scatter.3.cloned.1.call-update) | async-done | bytes 229392 | tf_op jit(solution)/shard_map/reduce_scatter | solution.py:35
  95.9 0.0 copy-done.2
  95.9 0.0 copy-done.1
  95.9 2.0 fusion.7
  97.9 0.0 all-gather.4.cloned.1.call-update
  97.9 0.0 all-gather.6.cloned.1.call-start
  98.0 0.7 all-gather.6.cloned.1.call-update
  98.7 0.0 all-gather.8.cloned.1.call-start
  98.7 0.5 all-gather.8.cloned.1.call-update
  99.2 0.0 reduce-scatter.5.cloned.1.call-start
  99.3 0.0 copy-done.3
  99.3 4.9 %all_gather.18 = bf16[128,512]{1,0:T(8,128)(2,1)S(1)} all-gather(bf16[64,512]{1,0:T(8,128)(2,1)S(1)} %copy-done.3), channel_id=1, replica_groups=mesh['gx'=16,'gy'=2] {'gy'}, dimensions={0}, use_global_device_ids=true | all-gather | bytes 196608 | tf_op jit(solution)/shard_map/all_gather | solution.py:32
  104.2 41.1 %all-gather.4.cloned.1.call-done = bf16[128,14336]{1,0:T(8,128)(2,1)} async-done(((bf16[8,14336]{1,0:T(8,128)(2,1)}), bf16[128,14336]{1,0:T(8,128)(2,1)}) %all-gather.4.cloned.1.call-update) | async-done | bytes 3670032 | tf_op jit(solution)/shard_map/all_gather | solution.py:39
  145.4 11.3 %fusion.12 = f32[128,512]{1,0:T(8,128)S(1)} fusion(bf16[128,14336]{1,0:T(8,128)(2,1)} %all-gather.4.cloned.1.call-done, bf16[512,14336]{1,0:T(8,128)(2,1)} %param.11), kind=kOutput, calls=%fused_computation.23 | convolution fusion | flops 1879048192 | bytes 18612224 | tf_op jit(solution)/shard_map/dot_general | solution.py:25
  156.7 38.4 %all-gather.6.cloned.1.call-done = bf16[128,14336]{1,0:T(8,128)(2,1)} async-done(((bf16[8,14336]{1,0:T(8,128)(2,1)}), bf16[128,14336]{1,0:T(8,128)(2,1)}) %all-gather.6.cloned.1.call-update) | async-done | bytes 3670032 | tf_op jit(solution)/shard_map/all_gather | solution.py:40
  195.1 11.9 %fusion.2 = bf16[128,512]{1,0:T(8,128)(2,1)} fusion(f32[128,512]{1,0:T(8,128)S(1)} %fusion.12, bf16[128,14336]{1,0:T(8,128)(2,1)} %all-gather.6.cloned.1.call-done, bf16[512,14336]{1,0:T(8,128)(2,1)} %param.12), kind=kOutput, calls=%fused_computation.7 | convolution fusion | flops 1879179264 | bytes 18743296 | tf_op jit(solution)/shard_map/dot_general | solution.py:25
  207.1 0.0 reduce-scatter.5.cloned.1.call-update
  207.1 0.0 copy-start
  207.1 10.0 %fusion = bf16[512,14336]{0,1:T(8,128)(2,1)} fusion(bf16[128,14336]{1,0:T(8,128)(2,1)} %all-gather.4.cloned.1.call-done, bf16[128,512]{1,0:T(8,128)(2,1)S(1)} %all_gather.18), kind=kOutput, calls=%fused_computation.3 | convolution fusion | flops 1886388224 | bytes 18481152 | tf_op jit(solution)/shard_map/dot_general | solution.py:19
  217.0 0.0 copy-done
  217.0 7.5 %fusion.1 = bf16[512,14336]{0,1:T(8,128)(2,1)} fusion(bf16[128,14336]{1,0:T(8,128)(2,1)S(1)} %copy-done, bf16[128,512]{1,0:T(8,128)(2,1)S(1)} %all_gather.18), kind=kOutput, calls=%fused_computation.4 | convolution fusion | flops 1886388224 | bytes 18481152 | tf_op jit(solution)/shard_map/dot_general | solution.py:19
  224.6 20.1 %all-gather.8.cloned.1.call-done = bf16[128,14336]{1,0:T(8,128)(2,1)} async-done(((bf16[8,14336]{1,0:T(8,128)(2,1)}), bf16[128,14336]{1,0:T(8,128)(2,1)}) %all-gather.8.cloned.1.call-update) | async-done | bytes 3670032 | tf_op jit(solution)/shard_map/all_gather | solution.py:41
  244.7 9.6 %convolution_convert_fusion = bf16[14336,512]{1,0:T(8,128)(2,1)} fusion(bf16[128,14336]{1,0:T(8,128)(2,1)} %all-gather.8.cloned.1.call-done, bf16[128,512]{1,0:T(8,128)(2,1)S(1)} %all_gather.15), kind=kOutput, calls=%fused_computation | convolution fusion | flops 1886388224 | bytes 18481152 | tf_op jit(solution)/shard_map/dot_general | solution.py:19
  254.3 19.9 %copy.11 = bf16[512,14336]{1,0:T(8,128)(2,1)} copy(bf16[512,14336]{0,1:T(8,128)(2,1)} %fusion) | data formatting | bytes 29360128
  274.2 19.9 %copy.12 = bf16[512,14336]{1,0:T(8,128)(2,1)} copy(bf16[512,14336]{0,1:T(8,128)(2,1)} %fusion.1) | data formatting | bytes 29360128
  294.1 0.0 reduce-scatter.5.cloned.1.call-done
Async XLA Ops:
  7.2 88.7 %copy-start.2 = (bf16[8,14336]{1,0:T(8,128)(2,1)S(1)}, bf16[8,14336]{1,0:T(8,128)(2,1)}, u32[]{:S(2)}) copy-start(bf16[8,14336]{1,0:T(8,128)(2,1)} %param.8) | copy-start | bytes 688132
  7.2 88.7 %copy-start.1 = (bf16[8,14336]{1,0:T(8,128)(2,1)S(1)}, bf16[8,14336]{1,0:T(8,128)(2,1)}, u32[]{:S(2)}) copy-start(bf16[8,14336]{1,0:T(8,128)(2,1)} %param.9) | copy-start | bytes 688132
  7.2 92.1 %copy-start.3 = (bf16[64,512]{1,0:T(8,128)(2,1)S(1)}, bf16[64,512]{1,0:T(8,128)(2,1)}, u32[]{:S(2)}) copy-start(bf16[64,512]{1,0:T(8,128)(2,1)} %param.7) | copy-start | bytes 196612
  7.2 88.7 %reduce-scatter.3.cloned.1.call-start = ((), (), s32[]{:S(2)}) async-start(), calls=%async_computation.2 | async-start | bytes 3899392 | tf_op jit(solution)/shard_map/reduce_scatter | solution.py:35
  25.3 120.0 %all-gather.4.cloned.1.call-start = ((), (), s32[]{:S(2)}) async-start(), calls=%async_computation.3 | async-start | bytes 3899392 | tf_op jit(solution)/shard_map/all_gather | solution.py:39
  97.9 97.2 %all-gather.6.cloned.1.call-start = ((), (), s32[]{:S(2)}) async-start(), calls=%async_computation.4 | async-start | bytes 3899392 | tf_op jit(solution)/shard_map/all_gather | solution.py:40
  98.7 146.0 %all-gather.8.cloned.1.call-start = ((), (), s32[]{:S(2)}) async-start(), calls=%async_computation.6 | async-start | bytes 3899392 | tf_op jit(solution)/shard_map/all_gather | solution.py:41
  99.2 194.9 %reduce-scatter.5.cloned.1.call-start = ((), (), s32[]{:S(2)}) async-start(), calls=%async_computation.5 | async-start | bytes 196608 | tf_op jit(solution)/shard_map/reduce_scatter | solution.py:48
  207.1 10.0 %copy-start = (bf16[128,14336]{1,0:T(8,128)(2,1)S(1)}, bf16[128,14336]{1,0:T(8,128)(2,1)}, u32[]{:S(2)}) copy-start(bf16[128,14336]{1,0:T(8,128)(2,1)} %all-gather.6.cloned.1.call-done) | copy-start | bytes 11010052
Sparse Core Ops, SparseCore 0:
  25.5 70.3 reduce-scatter.2
  99.0 46.3 all-gather.3
  148.5 46.5 all-gather.5
  198.1 46.5 all-gather.7
  247.4 9.2 reduce-scatter.4
where the time goes:
time: 302 us; the launch traced here: 301 us
  waiting for transfers between devices  171 us (57%)
  matrix products  62.2 us (21%)
  local copies, waits for them, and re-layouts  39.8 us (13%)
  between operations  13.8 us (5%)
  blocking collectives  11.2 us (4%)
    reduce_scatter x1, waiting for transfers between devices, per_device(): lax.psum_scatter(contract_cols(grad_rows, w_down).astype(jnp.bfloat16), '...  70.5 us
    all_gather x1, waiting for transfers between devices, per_device(): gate_piece = lax.all_gather(d_gate, 'gx', axis=0, tiled=True)  41.1 us
    unnamed x10, local copies, waits for them, and re-layouts  39.8 us
    all_gather x1, waiting for transfers between devices, per_device(): up_piece = lax.all_gather(d_up, 'gx', axis=0, tiled=True)  38.4 us
    dot_general x3, matrix products, contract_cols(): lax.dot_general(left, right, (((1,), (1,)), ((), ())), preferred_element_...  35.1 us
    dot_general x3, matrix products, contract_rows(): lax.dot_general(left, right, (((0,), (0,)), ((), ())), preferred_element_...  27.1 us
    all_gather x1, waiting for transfers between devices, per_device(): hidden_piece = lax.all_gather(hidden, 'gx', axis=0, tiled=True)  20.1 us
    all_gather x1, blocking collectives, per_device(): lax.all_gather(out_grad, 'gy', axis=0, tiled=True)  6.24 us
  transfers between devices with their start and end apart: 5, of which 4 were waited for; matrix products, arithmetic and copies ran while one was open for 30% of the time, Pallas kernels for 0%

commit v1 on v0

--- a/solution.py
+++ b/solution.py
@@ -37,8 +37,11 @@
     ).astype(jnp.float32)
     d_gate, d_up, hidden = swiglu_back(d_hidden, gate_pre, up_pre)
     gate_piece = lax.all_gather(d_gate, "gx", axis=0, tiled=True)
-    up_piece = lax.all_gather(d_up, "gx", axis=0, tiled=True)
-    hidden_piece = lax.all_gather(hidden, "gx", axis=0, tiled=True)
+    up_piece, hidden_piece = jnp.split(
+        lax.all_gather(jnp.concatenate([d_up, hidden], axis=1), "gx", axis=0, tiled=True),
+        [d_up.shape[1]],
+        axis=1,
+    )
     gate_total = contract_rows(input_rows, gate_piece)
     up_total = contract_rows(input_rows, up_piece)
     down_total = contract_rows(hidden_piece, grad_rows)

time: 302 us -> 275 us (0.911)
  waiting for transfers between devices: 171 us -> 141 us
    all_gather x2 -> x1, waiting for transfers between devices: 58.5 us -> 28.7 us  [per_device(): lax.all_gather(jnp.concatenate([d_up, hidden], axis=1), 'gx', axis=0, til...]
    unnamed x10 -> x8, local copies, waits for them, and re-layouts: 39.8 us -> 39.9 us
  transfers between devices with their start and end apart: 5 -> 4, of which waited for: 4 -> 3; matrix products, arithmetic and copies ran while one was open for 30% -> 30% of each run, Pallas kernels for 0% -> 0%
where the time goes in v1:
time: 275 us; the launch traced here: 273 us
  waiting for transfers between devices  141 us (51%)
  matrix products  64.6 us (23%)
  local copies, waits for them, and re-layouts  39.9 us (15%)
  between operations  13.8 us (5%)
  blocking collectives  11.4 us (4%)
    reduce_scatter x1, waiting for transfers between devices, per_device(): lax.psum_scatter(contract_cols(grad_rows, w_down).astype(jnp.bfloat16), '...  70.5 us
    all_gather x1, waiting for transfers between devices, per_device(): gate_piece = lax.all_gather(d_gate, 'gx', axis=0, tiled=True)  41.5 us
    unnamed x8, local copies, waits for them, and re-layouts  39.9 us
    dot_general x3, matrix products, contract_cols(): lax.dot_general(left, right, (((1,), (1,)), ((), ())), preferred_element_...  36 us
    all_gather x1, waiting for transfers between devices, per_device(): lax.all_gather(jnp.concatenate([d_up, hidden], axis=1), 'gx', axis=0, til...  28.7 us
    dot_general x3, matrix products, contract_rows(): lax.dot_general(left, right, (((0,), (0,)), ((), ())), preferred_element_...  28.6 us
    all_gather x1, blocking collectives, per_device(): lax.all_gather(out_grad, 'gy', axis=0, tiled=True)  6.24 us
  transfers between devices with their start and end apart: 4, of which 3 were waited for; matrix products, arithmetic and copies ran while one was open for 30% of the time, Pallas kernels for 0%

profile of v1, /device:TPU:0, one launch (start us, length us, event | category | flops | bytes accessed | tf_op | source)
XLA Modules:
  0.0 273.3 jit_solution(8901802857804301096)
XLA Ops:
  7.2 0.0 copy-start.1
  7.2 0.0 copy-start
  7.2 0.0 copy-start.2
  7.2 0.0 reduce-scatter.3.cloned.1.call-start
  7.2 6.2 %all_gather.12 = bf16[128,512]{1,0:T(8,128)(2,1)S(1)} all-gather(bf16[64,512]{1,0:T(8,128)(2,1)} %param.10), channel_id=1, replica_groups=mesh['gx'=16,'gy'=2] {'gy'}, dimensions={0}, use_global_device_ids=true | all-gather | bytes 196608 | tf_op jit(solution)/shard_map/all_gather | solution.py:33
  13.5 11.8 %convolution_convert_fusion.3 = bf16[128,14336]{1,0:T(8,128)(2,1)} fusion(bf16[128,512]{1,0:T(8,128)(2,1)S(1)} %all_gather.12, bf16[14336,512]{1,0:T(8,128)(2,1)} %param.13), kind=kOutput, calls=%fused_computation.5 | convolution fusion | flops 1880883200 | bytes 18481152 | tf_op jit(solution)/shard_map/dot_general | solution.py:25
  25.3 0.0 reduce-scatter.3.cloned.1.call-update
  25.3 0.0 all-gather.3.cloned.1.call-start
  25.4 70.5 %reduce-scatter.3.cloned.1.call-done = bf16[8,14336]{1,0:T(8,128)(2,1)} async-done(((bf16[128,14336]{1,0:T(8,128)(2,1)}), bf16[8,14336]{1,0:T(8,128)(2,1)}) %reduce-scatter.3.cloned.1.call-update) | async-done | bytes 229392 | tf_op jit(solution)/shard_map/reduce_scatter | solution.py:35
  95.9 0.0 copy-done.1
  95.9 0.0 copy-done
  95.9 1.9 fusion.12
  97.8 0.0 all-gather.3.cloned.1.call-update
  97.8 0.0 all-gather.5.cloned.1.call-start
  97.8 0.8 pad_maximum_fusion
  98.6 0.0 all-gather.5.cloned.1.call-update
  98.7 0.0 reduce-scatter.5.cloned.1.call-start
  98.7 0.0 copy-done.2
  98.7 5.1 %all_gather.15 = bf16[128,512]{1,0:T(8,128)(2,1)S(1)} all-gather(bf16[64,512]{1,0:T(8,128)(2,1)S(1)} %copy-done.2), channel_id=1, replica_groups=mesh['gx'=16,'gy'=2] {'gy'}, dimensions={0}, use_global_device_ids=true | all-gather | bytes 196608 | tf_op jit(solution)/shard_map/all_gather | solution.py:32
  103.9 41.5 %all-gather.3.cloned.1.call-done = bf16[128,14336]{1,0:T(8,128)(2,1)} async-done(((bf16[8,14336]{1,0:T(8,128)(2,1)}), bf16[128,14336]{1,0:T(8,128)(2,1)}) %all-gather.3.cloned.1.call-update) | async-done | bytes 3670032 | tf_op jit(solution)/shard_map/all_gather | solution.py:39
  145.4 9.6 %fusion = bf16[512,14336]{0,1:T(8,128)(2,1)} fusion(bf16[128,14336]{1,0:T(8,128)(2,1)} %all-gather.3.cloned.1.call-done, bf16[128,512]{1,0:T(8,128)(2,1)S(1)} %all_gather.15), kind=kOutput, calls=%fused_computation.3 | convolution fusion | flops 1886388224 | bytes 18481152 | tf_op jit(solution)/shard_map/dot_general | solution.py:19
  155.0 20.0 %copy.11 = bf16[512,14336]{1,0:T(8,128)(2,1)} copy(bf16[512,14336]{0,1:T(8,128)(2,1)} %fusion) | data formatting | bytes 29360128
  174.9 12.2 %fusion.21 = f32[128,512]{1,0:T(8,128)S(1)} fusion(bf16[128,14336]{1,0:T(8,128)(2,1)} %all-gather.3.cloned.1.call-done, bf16[512,14336]{1,0:T(8,128)(2,1)} %param.11), kind=kOutput, calls=%fused_computation.28 | convolution fusion | flops 1879048192 | bytes 18612224 | tf_op jit(solution)/shard_map/dot_general | solution.py:25
  187.2 28.7 %all-gather.5.cloned.1.call-done = bf16[128,28672]{1,0:T(8,128)(2,1)} async-done(((bf16[8,28672]{1,0:T(8,128)(2,1)}), bf16[128,28672]{1,0:T(8,128)(2,1)}) %all-gather.5.cloned.1.call-update) | async-done | bytes 7340048 | tf_op jit(solution)/shard_map/all_gather | solution.py:41
  215.8 12.0 %fusion.9 = bf16[128,512]{1,0:T(8,128)(2,1)} fusion(f32[128,512]{1,0:T(8,128)S(1)} %fusion.21, bf16[512,14336]{1,0:T(8,128)(2,1)} %param.12, bf16[128,28672]{1,0:T(8,128)(2,1)} %all-gather.5.cloned.1.call-done), kind=kOutput, calls=%fused_computation.11 | convolution fusion | flops 1879179264 | bytes 18743296 | tf_op jit(solution)/shard_map/dot_general | solution.py:25
  227.8 0.0 reduce-scatter.5.cloned.1.call-update
  227.8 9.4 %fusion.1 = bf16[512,14336]{0,1:T(8,128)(2,1)} fusion(bf16[128,512]{1,0:T(8,128)(2,1)S(1)} %all_gather.15, bf16[128,28672]{1,0:T(8,128)(2,1)} %all-gather.5.cloned.1.call-done), kind=kOutput, calls=%fused_computation.4 | convolution fusion | flops 1886388224 | bytes 18481152 | tf_op jit(solution)/shard_map/dot_general | solution.py:19
  237.2 9.6 %convolution_convert_fusion = bf16[14336,512]{1,0:T(8,128)(2,1)} fusion(bf16[128,512]{1,0:T(8,128)(2,1)S(1)} %all_gather.12, bf16[128,28672]{1,0:T(8,128)(2,1)} %all-gather.5.cloned.1.call-done), kind=kOutput, calls=%fused_computation | convolution fusion | flops 1886388224 | bytes 18481152 | tf_op jit(solution)/shard_map/dot_general | solution.py:19
  246.8 19.9 %copy.12 = bf16[512,14336]{1,0:T(8,128)(2,1)} copy(bf16[512,14336]{0,1:T(8,128)(2,1)} %fusion.1) | data formatting | bytes 29360128
  266.7 0.0 reduce-scatter.5.cloned.1.call-done
Async XLA Ops:
  7.2 88.7 %copy-start.1 = (bf16[8,14336]{1,0:T(8,128)(2,1)S(1)}, bf16[8,14336]{1,0:T(8,128)(2,1)}, u32[]{:S(2)}) copy-start(bf16[8,14336]{1,0:T(8,128)(2,1)} %param.9) | copy-start | bytes 688132
  7.2 88.7 %copy-start = (bf16[8,14336]{1,0:T(8,128)(2,1)S(1)}, bf16[8,14336]{1,0:T(8,128)(2,1)}, u32[]{:S(2)}) copy-start(bf16[8,14336]{1,0:T(8,128)(2,1)} %param.8) | copy-start | bytes 688132
  7.2 91.5 %copy-start.2 = (bf16[64,512]{1,0:T(8,128)(2,1)S(1)}, bf16[64,512]{1,0:T(8,128)(2,1)}, u32[]{:S(2)}) copy-start(bf16[64,512]{1,0:T(8,128)(2,1)} %param.7) | copy-start | bytes 196612
  7.2 88.7 %reduce-scatter.3.cloned.1.call-start = ((), (), s32[]{:S(2)}) async-start(), calls=%async_computation.2 | async-start | bytes 3899392 | tf_op jit(solution)/shard_map/reduce_scatter | solution.py:35
  25.3 120.0 %all-gather.3.cloned.1.call-start = ((), (), s32[]{:S(2)}) async-start(), calls=%async_computation.3 | async-start | bytes 3899392 | tf_op jit(solution)/shard_map/all_gather | solution.py:39
  97.8 118.0 %all-gather.5.cloned.1.call-start = ((), (), s32[]{:S(2)}) async-start(), calls=%async_computation.4 | async-start | bytes 7798784 | tf_op jit(solution)/shard_map/all_gather | solution.py:41
  98.7 168.1 %reduce-scatter.5.cloned.1.call-start = ((), (), s32[]{:S(2)}) async-start(), calls=%async_computation.5 | async-start | bytes 196608 | tf_op jit(solution)/shard_map/reduce_scatter | solution.py:51
Sparse Core Ops, SparseCore 0:
  25.5 70.3 reduce-scatter.2
  99.0 46.3 all-gather.2
  148.5 67.3 all-gather.4
  227.9 8.6 reduce-scatter.4
